TPU v7x, 32 devices: a whole 2x2x4 slice. The times are simulated.
32 devices in a mesh: group: 8 (over z, y), row: 2 (over x), col: 2 (over core).
Axes of the slice: x: 2, y: 2, z: 4, core: 2. Of those that a mesh axis runs over, the one named last changes fastest.
Arguments:
- tokens: bfloat16 [5120, 2048], P(('group', 'col'), 'row'), may hold values from -6 to 6
- lengths: int32 [24], P('group'), may hold values from 1 to 512, as said below
- norm_gain: float32 [2048], P('row'), may hold values from 0.25 to 1.75
- w_query: bfloat16 [2048, 2048], P('row', 'col'), may hold values from -0.125 to 0.125
- w_key: bfloat16 [2048, 1024], P('row', 'col'), may hold values from -0.125 to 0.125
- w_value: bfloat16 [2048, 1024], P('row', 'col'), may hold values from -0.125 to 0.125
- w_head_gate: bfloat16 [2048, 16], P('row', 'col'), may hold values from -0.25 to 0.25
- query_gain: float32 [128], replicated, may hold values from 1 to 2
- key_gain: float32 [128], replicated, may hold values from 1 to 2
- w_out: bfloat16 [2048, 2048], P('col', 'row'), may hold values from -1.5 to 1.5
- ffn_gain: float32 [2048], P('row'), may hold values from 0.25 to 1.75
- w_gate: bfloat16 [2048, 6144], P('row', 'col'), may hold values from -0.125 to 0.125
- w_up: bfloat16 [2048, 6144], P('row', 'col'), may hold values from -0.125 to 0.125
- w_down: bfloat16 [6144, 2048], P('col', 'row'), may hold values from -0.15625 to 0.15625
- grad_out: bfloat16 [5120, 2048], P(('group', 'col'), 'row'), may hold values from -6 to 6
Outputs:
- output: bfloat16 [5120, 2048], P(('group', 'col'), 'row')
- input_grad: float32 [5120, 2048], P(('group', 'col'), 'row')
- grad_norm_gain: float32 [2048], P('row')
- grad_w_query: float32 [2048, 2048], P('row', 'col')
- grad_w_key: float32 [2048, 1024], P('row', 'col')
- grad_w_value: float32 [2048, 1024], P('row', 'col')
- grad_w_head_gate: float32 [2048, 16], P('row', 'col')
- grad_query_gain: float32 [128], replicated
- grad_key_gain: float32 [128], replicated
- grad_w_out: float32 [2048, 2048], P('col', 'row')
- grad_ffn_gain: float32 [2048], P('row')
- grad_w_gate: float32 [2048, 6144], P('row', 'col')
- grad_w_up: float32 [2048, 6144], P('row', 'col')
- grad_w_down: float32 [6144, 2048], P('col', 'row')
Inputs may be any that keep to these rules, and one draw needn't show every extreme that they name: Each group's 3 entries are the lengths of its sequences in token order; they sum to 640.
All inputs are finite; a program needn't handle non-finite values.
Results may differ from a plain program's by a relative error of at most 0.024.
Values may be sent and summed in bfloat16 or wider, within the bound.
A program may use at most 256 MiB of HBM per device.

v0:
```python
import jax
import jax.numpy as jnp
from jax import lax
from jax.sharding import PartitionSpec as P

EPS = 1e-06
THETA = 1000000.0
NEGATIVE = -1e30


def places(lengths_group, count):
    ends = jnp.cumsum(lengths_group)
    index = jnp.arange(count, dtype=jnp.int32)
    passed = (index[:, None] >= ends[None, :]).astype(jnp.int32)
    segment = jnp.sum(passed, axis=1)
    place = index - jnp.sum(passed * lengths_group[None, :], axis=1)
    return (segment, place)


def rope_tables(place, width):
    half = width // 2
    freq = THETA ** (-(jnp.arange(half, dtype=jnp.float32) * 2.0 / width))
    angle = place.astype(jnp.float32)[:, None] * freq[None, :]
    cosines = jnp.concatenate([jnp.cos(angle), jnp.cos(angle)], axis=1)
    sines = jnp.concatenate([jnp.sin(angle), jnp.sin(angle)], axis=1)
    return (cosines, sines)


def rotate(values, cosines, sines):
    half = values.shape[-1] // 2
    turned = jnp.concatenate([-values[..., half:], values[..., :half]], axis=-1)
    return values * cosines + turned * sines


def unrotate(grads, cosines, sines):
    half = grads.shape[-1] // 2
    scaled = grads * sines
    return grads * cosines + jnp.concatenate([scaled[..., half:], -scaled[..., :half]], axis=-1)


def head_norm_back(d_normed, raw_values, inverse, gain):
    scaled = d_normed * gain
    gain_part = jnp.sum(d_normed * raw_values * inverse, axis=(0, 1))
    d_raw = inverse * scaled - raw_values * inverse**3 * jnp.mean(
        scaled * raw_values, axis=-1, keepdims=True
    )
    return (d_raw, gain_part)


def across_features(values):
    return lax.psum(values, "row")


def gather_tokens(values):
    return lax.all_gather(values, "col", axis=0, tiled=True)


def gather_blocks(values):
    return lax.all_gather(values, "row", axis=0, tiled=True)


def reduce_rows(term, rows):
    return lax.psum_scatter(
        term(jnp.int32(0), lax.axis_size("row") * rows), "row", scatter_dimension=0, tiled=True
    )


def reduce_cols(term, rows):
    return lax.psum_scatter(
        term(jnp.int32(0), lax.axis_size("col") * rows).astype(jnp.bfloat16),
        "col",
        scatter_dimension=0,
        tiled=True,
    ).astype(jnp.float32)


def masked_scores(block_query, block_segment, block_place, key_rows, segment, place, scale):
    scores = (
        jnp.einsum("qkgd,skd->kgqs", block_query, key_rows, preferred_element_type=jnp.float32)
        * scale
    )
    allowed = (block_segment[:, None] == segment[None, :]) & (
        place[None, :] <= block_place[:, None]
    )
    return jnp.where(allowed, scores, NEGATIVE)


def body(
    tokens,
    lengths,
    norm_gain,
    w_query,
    w_key,
    w_value,
    w_head_gate,
    query_gain,
    key_gain,
    w_out,
    ffn_gain,
    w_gate,
    w_up,
    w_down,
    grad_out,
):
    row_count = lax.axis_size("row")
    col_count = lax.axis_size("col")
    tok_dev, d_loc = tokens.shape
    group_tok = tok_dev * col_count
    bin_rows = group_tok // row_count
    head_dim = query_gain.shape[0]
    q_cols = w_query.shape[1]
    kv_cols = w_key.shape[1]
    heads_loc = q_cols // head_dim
    kv_loc = kv_cols // head_dim
    share = heads_loc // kv_loc
    width = d_loc * row_count
    ff_loc = w_gate.shape[1]
    scale = head_dim ** (-0.5)
    blocks = bin_rows // bin_rows
    row_at = lax.axis_index("row")
    position = jnp.arange(group_tok, dtype=jnp.int32)
    order = position % bin_rows * row_count + position // bin_rows
    inverse = position % row_count * bin_rows + position // row_count
    segment, place = places(lengths, group_tok)
    all_segment = segment[order]
    all_place = place[order]
    bin_segment = lax.dynamic_slice_in_dim(all_segment, row_at * bin_rows, bin_rows)
    bin_place = lax.dynamic_slice_in_dim(all_place, row_at * bin_rows, bin_rows)
    x_in = tokens.astype(jnp.float32)
    inverse_one = lax.rsqrt(across_features(jnp.sum(x_in * x_in, axis=1)) / width + EPS)
    normed_one = (x_in * inverse_one[:, None] * norm_gain).astype(jnp.bfloat16)
    gathered_one = gather_tokens(normed_one)
    permuted = gathered_one[order]
    w_first = jnp.concatenate([w_query, w_key, w_value, w_head_gate], axis=1)

    def first_term(start, row_total):
        return jnp.dot(permuted, w_first, preferred_element_type=jnp.float32)

    projected = reduce_rows(first_term, bin_rows)
    raw_query = projected[:, :q_cols].reshape(bin_rows, heads_loc, head_dim)
    raw_key = projected[:, q_cols : q_cols + kv_cols].reshape(bin_rows, kv_loc, head_dim)
    raw_value = projected[:, q_cols + kv_cols : q_cols + 2 * kv_cols].reshape(
        bin_rows, kv_loc, head_dim
    )
    logit = projected[:, q_cols + 2 * kv_cols :]
    query_inverse = lax.rsqrt(jnp.mean(raw_query * raw_query, axis=-1, keepdims=True) + EPS)
    key_inverse = lax.rsqrt(jnp.mean(raw_key * raw_key, axis=-1, keepdims=True) + EPS)
    cosines, sines = rope_tables(bin_place, head_dim)
    cos_heads = cosines[:, None, :]
    sin_heads = sines[:, None, :]
    query = rotate(raw_query * query_inverse * query_gain, cos_heads, sin_heads).astype(
        jnp.bfloat16
    )
    key_local = rotate(raw_key * key_inverse * key_gain, cos_heads, sin_heads).astype(jnp.bfloat16)
    value_local = raw_value.astype(jnp.bfloat16)
    key_rows, value_rows = (
        lax.all_gather(key_local, "row", axis=0, tiled=True),
        lax.all_gather(value_local, "row", axis=0, tiled=True),
    )
    query_blocks = query.reshape(blocks, bin_rows, kv_loc, share, head_dim)
    segment_blocks = bin_segment.reshape(blocks, bin_rows)
    place_blocks = bin_place.reshape(blocks, bin_rows)

    def forward_block(item):
        block_query, block_segment, block_place = item
        scores = masked_scores(
            block_query, block_segment, block_place, key_rows, all_segment, all_place, scale
        )
        top_score = jnp.max(scores, axis=-1, keepdims=True)
        raised = jnp.exp(scores - top_score)
        total = jnp.sum(raised, axis=-1, keepdims=True)
        probs = (raised / total).astype(jnp.bfloat16)
        result = jnp.einsum("kgqs,skd->qkgd", probs, value_rows, preferred_element_type=jnp.float32)
        return (result, top_score[..., 0] + jnp.log(total[..., 0]))

    attended_blocks, logsum_blocks = lax.map(
        forward_block, (query_blocks, segment_blocks, place_blocks)
    )
    attended = attended_blocks.reshape(bin_rows, heads_loc, head_dim)
    gate_sigmoid = jax.nn.sigmoid(logit)
    gated = (attended * gate_sigmoid[:, :, None]).reshape(bin_rows, q_cols).astype(jnp.bfloat16)
    gathered_gated = gather_blocks(gated)

    def out_term(start, row_total):
        return jnp.dot(gathered_gated[inverse], w_out, preferred_element_type=jnp.float32)

    attn_branch = reduce_cols(out_term, tok_dev)
    resid = x_in + attn_branch
    inverse_two = lax.rsqrt(across_features(jnp.sum(resid * resid, axis=1)) / width + EPS)
    normed_two = (resid * inverse_two[:, None] * ffn_gain).astype(jnp.bfloat16)
    gathered_two = gather_tokens(normed_two)
    w_pair = jnp.concatenate([w_gate, w_up], axis=1)
    pair_value = lax.psum_scatter(
        jnp.dot(gathered_two, w_pair, preferred_element_type=jnp.float32).astype(jnp.bfloat16),
        "row",
        scatter_dimension=0,
        tiled=True,
    ).astype(jnp.float32)
    gate_part = pair_value[:, :ff_loc]
    up_part = pair_value[:, ff_loc:]
    gate_sig = jax.nn.sigmoid(gate_part)
    silu_part = gate_part * gate_sig
    inner = (silu_part * up_part).astype(jnp.bfloat16)
    gathered_inner = gather_blocks(inner)

    def down_term(start, row_total):
        return jnp.dot(gathered_inner, w_down, preferred_element_type=jnp.float32)

    branch = reduce_cols(down_term, tok_dev)
    output = (resid + branch).astype(jnp.bfloat16)
    d_top = grad_out.astype(jnp.float32)
    gathered_grad = gather_tokens(grad_out)
    grad_down = jnp.einsum(
        "tf,td->fd", gathered_inner, gathered_grad, preferred_element_type=jnp.float32
    )

    def inner_term(start, row_total):
        return jnp.einsum("td,fd->tf", gathered_grad, w_down, preferred_element_type=jnp.float32)

    d_inner = reduce_rows(inner_term, bin_rows)
    d_gate = d_inner * up_part * (gate_sig * (1.0 + gate_part * (1.0 - gate_sig)))
    d_up = d_inner * silu_part
    d_pair = jnp.concatenate([d_gate, d_up], axis=1).astype(jnp.bfloat16)
    gathered_pair = lax.all_gather(d_pair, "row", axis=0, tiled=True)
    whole_grad = jnp.einsum(
        "td,tf->df", gathered_two, gathered_pair, preferred_element_type=jnp.float32
    )
    grad_gate = whole_grad[:, :ff_loc]
    grad_up = whole_grad[:, ff_loc:]

    def norm_term(start, row_total):
        return jnp.einsum("tf,df->td", gathered_pair, w_pair, preferred_element_type=jnp.float32)

    d_normed_two = reduce_cols(norm_term, tok_dev)
    ffn_gain_part = jnp.sum(d_normed_two * resid * inverse_two[:, None], axis=0)
    scaled_two = d_normed_two * ffn_gain
    inner_two = across_features(jnp.sum(scaled_two * resid, axis=1))
    d_resid = (
        d_top
        + inverse_two[:, None] * scaled_two
        - resid * (inverse_two**3 * inner_two / width)[:, None]
    )
    d_branch = d_resid.astype(jnp.bfloat16)
    gathered_branch = gather_tokens(d_branch)
    permuted_branch = gathered_branch[order]
    grad_out_w = jnp.einsum(
        "tq,td->qd", gathered_gated, permuted_branch, preferred_element_type=jnp.float32
    )

    def gated_term(start, row_total):
        return jnp.einsum("td,qd->tq", permuted_branch, w_out, preferred_element_type=jnp.float32)

    d_gated = reduce_rows(gated_term, bin_rows).reshape(bin_rows, heads_loc, head_dim)
    d_attended = (d_gated * gate_sigmoid[:, :, None]).astype(jnp.bfloat16)
    d_logit = jnp.sum(d_gated * attended, axis=-1) * gate_sigmoid * (1.0 - gate_sigmoid)
    d_attended_blocks = d_attended.reshape(blocks, bin_rows, kv_loc, share, head_dim)

    def backward_block(carry, item):
        d_key_sum, d_value_sum = carry
        block_query, block_segment, block_place, block_grad, block_logsum = item
        scores = masked_scores(
            block_query, block_segment, block_place, key_rows, all_segment, all_place, scale
        )
        probs = jnp.exp(scores - block_logsum[..., None])
        d_probs = jnp.einsum(
            "qkgd,skd->kgqs", block_grad, value_rows, preferred_element_type=jnp.float32
        )
        d_scores = (probs * (d_probs - jnp.sum(d_probs * probs, axis=-1, keepdims=True))).astype(
            jnp.bfloat16
        )
        d_query_block = (
            jnp.einsum("kgqs,skd->qkgd", d_scores, key_rows, preferred_element_type=jnp.float32)
            * scale
        )
        d_key_sum = (
            d_key_sum
            + jnp.einsum(
                "kgqs,qkgd->skd", d_scores, block_query, preferred_element_type=jnp.float32
            )
            * scale
        )
        d_value_sum = d_value_sum + jnp.einsum(
            "kgqs,qkgd->skd",
            probs.astype(jnp.bfloat16),
            block_grad,
            preferred_element_type=jnp.float32,
        )
        return ((d_key_sum, d_value_sum), d_query_block)

    zero_rows = jnp.zeros((group_tok, kv_loc, head_dim), jnp.float32)
    (d_key_all, d_value_all), d_query_blocks = lax.scan(
        backward_block,
        (zero_rows, zero_rows),
        (query_blocks, segment_blocks, place_blocks, d_attended_blocks, logsum_blocks),
    )
    d_keys, d_values = (
        lax.psum_scatter(
            d_key_all.astype(jnp.bfloat16), "row", scatter_dimension=0, tiled=True
        ).astype(jnp.float32),
        lax.psum_scatter(
            d_value_all.astype(jnp.bfloat16), "row", scatter_dimension=0, tiled=True
        ).astype(jnp.float32),
    )
    d_query = d_query_blocks.reshape(bin_rows, heads_loc, head_dim)
    d_raw_query, query_gain_part = head_norm_back(
        unrotate(d_query, cos_heads, sin_heads), raw_query, query_inverse, query_gain
    )
    d_raw_key, key_gain_part = head_norm_back(
        unrotate(d_keys, cos_heads, sin_heads), raw_key, key_inverse, key_gain
    )
    d_projected = jnp.concatenate(
        [
            d_raw_query.reshape(bin_rows, q_cols),
            d_raw_key.reshape(bin_rows, kv_cols),
            d_values.reshape(bin_rows, kv_cols),
            d_logit,
        ],
        axis=1,
    ).astype(jnp.bfloat16)
    gathered_first = gather_blocks(d_projected)
    grad_first = jnp.einsum(
        "td,tc->dc", permuted, gathered_first, preferred_element_type=jnp.float32
    )

    def first_back_term(start, row_total):
        return jnp.einsum(
            "tc,dc->td", gathered_first[inverse], w_first, preferred_element_type=jnp.float32
        )

    d_normed_one = reduce_cols(first_back_term, tok_dev)
    norm_gain_part = jnp.sum(d_normed_one * x_in * inverse_one[:, None], axis=0)
    scaled_one = d_normed_one * norm_gain
    inner_one = across_features(jnp.sum(scaled_one * x_in, axis=1))
    input_grad = (
        d_resid
        + inverse_one[:, None] * scaled_one
        - x_in * (inverse_one**3 * inner_one / width)[:, None]
    )
    grad_norm_gain, grad_ffn_gain = lax.psum((norm_gain_part, ffn_gain_part), ("group", "col"))
    grad_query_gain, grad_key_gain = lax.psum(
        (query_gain_part, key_gain_part), ("group", "row", "col")
    )
    grad_query = grad_first[:, :q_cols]
    grad_key = grad_first[:, q_cols : q_cols + kv_cols]
    grad_value = grad_first[:, q_cols + kv_cols : q_cols + 2 * kv_cols]
    grad_head_gate = grad_first[:, q_cols + 2 * kv_cols :]
    summed = (
        lax.psum(grad_query.astype(jnp.bfloat16), "group").astype(jnp.float32),
        lax.psum(grad_key.astype(jnp.bfloat16), "group").astype(jnp.float32),
        lax.psum(grad_value.astype(jnp.bfloat16), "group").astype(jnp.float32),
        lax.psum(grad_head_gate.astype(jnp.bfloat16), "group").astype(jnp.float32),
        lax.psum(grad_out_w.astype(jnp.bfloat16), "group").astype(jnp.float32),
        lax.psum(grad_gate.astype(jnp.bfloat16), "group").astype(jnp.float32),
        lax.psum(grad_up.astype(jnp.bfloat16), "group").astype(jnp.float32),
        lax.psum(grad_down.astype(jnp.bfloat16), "group").astype(jnp.float32),
    )
    return (
        output,
        input_grad,
        grad_norm_gain,
        summed[0],
        summed[1],
        summed[2],
        summed[3],
        grad_query_gain,
        grad_key_gain,
        summed[4],
        grad_ffn_gain,
        summed[5],
        summed[6],
        summed[7],
    )


def solution(mesh):
    in_specs = (
        P(("group", "col"), "row"),
        P("group"),
        P("row"),
        P("row", "col"),
        P("row", "col"),
        P("row", "col"),
        P("row", "col"),
        P(),
        P(),
        P("col", "row"),
        P("row"),
        P("row", "col"),
        P("row", "col"),
        P("col", "row"),
        P(("group", "col"), "row"),
    )
    out_specs = (
        P(("group", "col"), "row"),
        P(("group", "col"), "row"),
        P("row"),
        P("row", "col"),
        P("row", "col"),
        P("row", "col"),
        P("row", "col"),
        P(),
        P(),
        P("col", "row"),
        P("row"),
        P("row", "col"),
        P("row", "col"),
        P("col", "row"),
    )
    return jax.shard_map(body, mesh=mesh, in_specs=in_specs, out_specs=out_specs, check_vma=False)
```

profile of v0, /device:TPU:0, one launch (start us, length us, event | category | flops | bytes accessed | tf_op | source)
XLA Modules:
  0.0 1673.6 jit_solution(9687963277787072502)
XLA Ops:
  18.3 10.4 all-gather.9.cloned.1.call-done
  34.1 8.5 fusion.52
  52.2 60.9 %reduce-scatter.28.cloned.1.call-done = f32[320,2056]{1,0:T(8,128)} async-done(((f32[640,2056]{1,0:T(8,128)}), f32[320,2056]{1,0:T(8,128)}) %reduce-scatter.28.cloned.1.call-update) | async-done | bytes 2631696 | tf_op jit(solution)/shard_map/reduce_scatter | solution.py:63
  134.4 10.9 all_gather.31
  149.0 10.0 all_gather.32
  185.8 25.1 %all-gather.11.cloned.1.call-done = bf16[640,1024]{1,0:T(8,128)(2,1)} async-done(((bf16[320,1024]{1,0:T(8,128)(2,1)}), bf16[640,1024]{1,0:T(8,128)(2,1)}) %all-gather.11.cloned.1.call-update) | async-done | bytes 1310736 | tf_op jit(solution)/shard_map/all_gather | solution.py:59
  220.8 8.9 reduce-scatter.12.cloned.1.call-done
  245.0 6.4 constant_dynamic-update-slice_fusion
  251.4 15.2 convolution_convert_fusion.1
  266.7 10.7 fusion.84
  277.4 84.6 %reduce-scatter.14.cloned.1.call-done = bf16[320,6144]{1,0:T(8,128)(2,1)} async-done(((bf16[640,6144]{1,0:T(8,128)(2,1)}), bf16[320,6144]{1,0:T(8,128)(2,1)}) %reduce-scatter.14.cloned.1.call-update) | async-done | bytes 3932176 | tf_op jit(solution)/shard_map/reduce_scatter | solution.py:193
  368.3 90.8 %reduce-scatter.18.cloned.1.call-done = f32[320,3072]{1,0:T(8,128)} async-done(((f32[640,3072]{1,0:T(8,128)}), f32[320,3072]{1,0:T(8,128)}) %reduce-scatter.18.cloned.1.call-update) | async-done | bytes 3932176 | tf_op jit(solution)/shard_map/reduce_scatter | solution.py:63
  459.1 6.7 multiply_convert_fusion.1
  468.5 97.8 %all-gather.19.cloned.1.call-done = bf16[640,6144]{1,0:T(8,128)(2,1)} async-done(((bf16[320,6144]{1,0:T(8,128)(2,1)}), bf16[640,6144]{1,0:T(8,128)(2,1)}) %all-gather.19.cloned.1.call-update) | async-done | bytes 7864336 | tf_op jit(solution)/shard_map/all_gather | solution.py:224
  566.3 14.4 convolution_convert_fusion.6
  580.8 8.9 reduce-scatter.20.cloned.1.call-done
  599.3 10.7 all-gather.21.cloned.1.call-done
  626.7 32.6 %reduce-scatter.22.cloned.1.call-done = f32[320,1024]{1,0:T(8,128)} async-done(((f32[640,1024]{1,0:T(8,128)}), f32[320,1024]{1,0:T(8,128)}) %reduce-scatter.22.cloned.1.call-update) | async-done | bytes 1310736 | tf_op jit(solution)/shard_map/reduce_scatter | solution.py:63
  711.1 12.1 reduce-scatter.24.cloned.1.call-done
  728.9 40.4 %all-gather.23.cloned.1.call-done = bf16[640,2056]{1,0:T(8,128)(2,1)} async-done(((bf16[320,2056]{1,0:T(8,128)(2,1)}), bf16[640,2056]{1,0:T(8,128)(2,1)}) %all-gather.23.cloned.1.call-update) | async-done | bytes 2631696 | tf_op jit(solution)/shard_map/all_gather | solution.py:59
  769.3 9.3 gather_fusion.5
  778.6 7.7 convolution_convert_fusion.5
  786.4 38.8 %all-gather.15.cloned.1.call-done = bf16[640,3072]{1,0:T(8,128)(2,1)} async-done(((bf16[320,3072]{1,0:T(8,128)(2,1)}), bf16[640,3072]{1,0:T(8,128)(2,1)}) %all-gather.15.cloned.1.call-update) | async-done | bytes 3932176 | tf_op jit(solution)/shard_map/all_gather | solution.py:59
  825.2 9.3 convolution_convert_fusion.7
  834.9 9.5 convolution_convert_fusion.2
  844.5 14.4 convolution_convert_fusion
  875.1 44.0 %all-reduce.1 = (f32[128]{0:T(128)}, f32[128]{0:T(128)}) all-reduce(f32[128]{0:T(128)S(1)} %bitcast_reduce_fusion, f32[128]{0:T(128)S(1)} %get-tuple-element.197), channel_id=1, replica_groups=mesh['group'=8,'row'=2,'col'=2] {'group','row','col'}, use_global_device_ids=true, to_apply=%region_37.38 | all-reduce | flops 256 | bytes 2048 | tf_op jit(solution)/shard_map/psum | solution.py:340
  919.1 37.7 %psum.120 = bf16[1024,8]{0,1:T(8,128)(2,1)S(1)} all-reduce(bf16[1024,8]{0,1:T(8,128)(2,1)S(1)} %slice-done.6), channel_id=1, replica_groups=mesh['group'=8,'row'=2,'col'=2] {'group'}, use_global_device_ids=true, to_apply=%region_34.35 | all-reduce | flops 8192 | bytes 32768 | tf_op jit(solution)/shard_map/psum | solution.py:351
  964.0 34.1 %all-reduce.2 = (f32[1024]{0:T(1024)}, f32[1024]{0:T(1024)}) all-reduce(f32[1024]{0:T(1024)S(1)} %get-tuple-element.199, f32[1024]{0:T(1024)S(1)} %get-tuple-element.195), channel_id=1, replica_groups=mesh['group'=8,'row'=2,'col'=2] {'group','col'}, use_global_device_ids=true, to_apply=%region_30.31 | all-reduce | flops 2048 | bytes 16384 | tf_op jit(solution)/shard_map/psum | solution.py:339
  1001.6 632.3 %all-reduce.9.cloned.1.call-done = (bf16[1024,1024]{0,1:T(8,128)(2,1)}, bf16[1024,512]{0,1:T(8,128)(2,1)}, bf16[1024,512]{0,1:T(8,128)(2,1)}, bf16[1024,1024]{1,...) async-done(((bf16[1024,1024]{0,1:T(8,128)(2,1)}, bf16[1024,512]{0,1:T(8,128)(2,1)}, ...) | async-done | bytes 25165840 | tf_op jit(solution)/shard_map/psum | solution.py:348
  1644.7 9.4 convert_element_type.179
  1654.1 6.4 convert_element_type.180
  (313 shorter events, 239.2 us)
Async XLA Ops:
  7.2 209.6 %copy-start = (bf16[1024,1024]{1,0:T(8,128)(2,1)S(1)}, bf16[1024,1024]{1,0:T(8,128)(2,1)}, u32[]{:S(2)}) copy-start(bf16[1024,1024]{1,0:T(8,128)(2,1)} %param.24) | copy-start | bytes 6291460
  7.2 21.5 %all-gather.9.cloned.1.call-start = ((), (), s32[]{:S(2)}) async-start(), calls=%async_computation.9 | async-start | bytes 1966080 | tf_op jit(solution)/shard_map/all_gather | solution.py:55
  17.3 95.9 %reduce-scatter.28.cloned.1.call-start = ((), (), s32[]{:S(2)}) async-start(), calls=%async_computation.25 | async-start | bytes 8355840 | tf_op jit(solution)/shard_map/reduce_scatter | solution.py:63
  42.6 168.3 %all-gather.11.cloned.1.call-start = ((), (), s32[]{:S(2)}) async-start(), calls=%async_computation.10 | async-start | bytes 1966080 | tf_op jit(solution)/shard_map/all_gather | solution.py:59
  128.6 16.6 copy-start.36
  130.6 16.8 %copy-start.58 = (f32[128]{0:T(128)S(1)}, f32[128]{0:T(128)}, u32[]{:S(2)}) copy-start(f32[128]{0:T(128)} %param.23) | copy-start | bytes 1540
  185.7 43.9 %reduce-scatter.12.cloned.1.call-start = ((), (), s32[]{:S(2)}) async-start(), calls=%async_computation.11 | async-start | bytes 1966080 | tf_op jit(solution)/shard_map/reduce_scatter | solution.py:69
  220.7 30.7 %all-gather.13.cloned.1.call-start = ((), (), s32[]{:S(2)}) async-start(), calls=%async_computation.12 | async-start | bytes 1966080 | tf_op jit(solution)/shard_map/all_gather | solution.py:55
  238.2 28.5 %all-gather.17.cloned.1.call-start = ((), (), s32[]{:S(2)}) async-start(), calls=%async_computation.16 | async-start | bytes 1966080 | tf_op jit(solution)/shard_map/all_gather | solution.py:55
  238.8 123.3 %reduce-scatter.14.cloned.1.call-start = ((), (), s32[]{:S(2)}) async-start(), calls=%async_computation.13 | async-start | bytes 11796480 | tf_op jit(solution)/shard_map/reduce_scatter | solution.py:193
  266.6 192.5 %reduce-scatter.18.cloned.1.call-start = ((), (), s32[]{:S(2)}) async-start(), calls=%async_computation.17 | async-start | bytes 11796480 | tf_op jit(solution)/shard_map/reduce_scatter | solution.py:63
  277.4 288.9 %all-gather.19.cloned.1.call-start = ((), (), s32[]{:S(2)}) async-start(), calls=%async_computation.18 | async-start | bytes 11796480 | tf_op jit(solution)/shard_map/all_gather | solution.py:224
  468.0 121.6 %reduce-scatter.20.cloned.1.call-start = ((), (), s32[]{:S(2)}) async-start(), calls=%async_computation.19 | async-start | bytes 1966080 | tf_op jit(solution)/shard_map/reduce_scatter | solution.py:69
  580.7 29.3 %all-gather.21.cloned.1.call-start = ((), (), s32[]{:S(2)}) async-start(), calls=%async_computation.20 | async-start | bytes 1966080 | tf_op jit(solution)/shard_map/all_gather | solution.py:55
  599.2 60.0 %reduce-scatter.22.cloned.1.call-start = ((), (), s32[]{:S(2)}) async-start(), calls=%async_computation.21 | async-start | bytes 3932160 | tf_op jit(solution)/shard_map/reduce_scatter | solution.py:63
  620.3 88.9 %all-reduce.7.cloned.1.call-start = ((), (), s32[]{:S(2)}) async-start(), calls=%async_computation.26 | async-start | bytes 1310720
  672.8 50.3 %reduce-scatter.24.cloned.1.call-start = ((), (), s32[]{:S(2)}) async-start(), calls=%async_computation.22 | async-start | bytes 983040 | tf_op jit(solution)/shard_map/reduce_scatter | solution.py:297
  695.8 73.5 %all-gather.23.cloned.1.call-start = ((), (), s32[]{:S(2)}) async-start(), calls=%async_computation.23 | async-start | bytes 4177920 | tf_op jit(solution)/shard_map/all_gather | solution.py:59
  704.8 18.4 %copy-start.32 = (f32[320,128]{1,0:T(8,128)S(1)}, f32[320,128]{1,0:T(8,128)}, u32[]{:S(2)}) copy-start(f32[320,128]{1,0:T(8,128)} %copy.217) | copy-start | bytes 491524
  728.3 96.9 %all-gather.15.cloned.1.call-start = ((), (), s32[]{:S(2)}) async-start(), calls=%async_computation.14 | async-start | bytes 5898240 | tf_op jit(solution)/shard_map/all_gather | solution.py:59
  728.9 49.8 %copy-start.50 = (bf16[1024,8]{1,0:T(8,128)(2,1)S(1)}, bf16[1024,8]{1,0:T(8,128)(2,1)}, u32[]{:S(2)}) copy-start(bf16[1024,8]{1,0:T(8,128)(2,1)} %copy.209) | copy-start | bytes 49156
  728.9 49.7 %copy-start.62 = (bf16[1024,512]{1,0:T(8,128)(2,1)S(1)}, bf16[1024,512]{1,0:T(8,128)(2,1)}, u32[]{:S(2)}) copy-start(bf16[1024,512]{1,0:T(8,128)(2,1)} %param.20) | copy-start | bytes 3145732
  728.9 228.6 %reduce-scatter.26.cloned.1.call-start = ((), (), s32[]{:S(2)}) async-start(), calls=%async_computation.24 | async-start | bytes 1966080 | tf_op jit(solution)/shard_map/reduce_scatter | solution.py:69
  786.3 211.8 %reduce-scatter.16.cloned.1.call-start = ((), (), s32[]{:S(2)}) async-start(), calls=%async_computation.15 | async-start | bytes 1966080 | tf_op jit(solution)/shard_map/reduce_scatter | solution.py:69
  834.5 799.4 %all-reduce.9.cloned.1.call-start = ((), (), s32[]{:S(2)}) async-start(), calls=%async_computation.27 | async-start | bytes 50331648 | tf_op jit(solution)/shard_map/psum | solution.py:348
  875.0 44.1 %slice-start.6 = ((bf16[1024,2056]{0,1:T(8,128)(2,1)}), bf16[1024,8]{0,1:T(8,128)(2,1)S(1)}, s32[]{:S(2)}) async-start(bf16[1024,2056]{0,1:T(8,128)(2,1)} %copy-done.25), calls=%async_computation.34 | async-start | bytes 32768 | tf_op jit(solution)/shard_map/slice | solution.py:346
  875.0 82.4 %copy-start.52 = (f32[1024]{0:T(1024)S(1)}, f32[1024]{0:T(1024)}, u32[]{:S(2)}) copy-start(f32[1024]{0:T(1024)} %param.17) | copy-start | bytes 12292
  875.0 82.4 %copy-start.54 = (f32[320]{0:T(512)S(1)}, f32[320]{0:T(512)}, u32[]{:S(2)}) copy-start(f32[320]{0:T(512)} %copy-done.53) | copy-start | bytes 3844
  875.0 123.0 %copy-start.56 = (f32[320]{0:T(512)S(1)}, f32[320]{0:T(512)}, u32[]{:S(2)}) copy-start(f32[320]{0:T(512)} %copy-done.55) | copy-start | bytes 3844
  875.0 123.1 %copy-start.18 = (bf16[320,1024]{1,0:T(8,128)(2,1)S(1)}, bf16[320,1024]{1,0:T(8,128)(2,1)}, u32[]{:S(2)}) copy-start(bf16[320,1024]{1,0:T(8,128)(2,1)} %reduce-scatter.20.cloned.1.call-done) | copy-start | bytes 1966084
  875.1 123.0 %copy-start.10 = (bf16[320,1024]{1,0:T(8,128)(2,1)S(1)}, bf16[320,1024]{1,0:T(8,128)(2,1)}, u32[]{:S(2)}) copy-start(bf16[320,1024]{1,0:T(8,128)(2,1)} %reduce-scatter.12.cloned.1.call-done) | copy-start | bytes 1966084
  875.1 123.0 %copy-start.17 = (bf16[320,1024]{1,0:T(8,128)(2,1)S(1)}, bf16[320,1024]{1,0:T(8,128)(2,1)}, u32[]{:S(2)}) copy-start(bf16[320,1024]{1,0:T(8,128)(2,1)} %param.29) | copy-start | bytes 1966084
  (58 other events, 243.9 us)
Sparse Core Ops, SparseCore 0:
  17.4 11.2 all-gather.8
  42.7 70.4 reduce-scatter.27
  185.8 24.9 all-gather.10
  220.9 8.7 reduce-scatter.11
  238.3 10.6 all-gather.12
  250.5 10.5 all-gather.16
  266.7 95.2 reduce-scatter.13
  364.9 94.1 reduce-scatter.17
  468.1 98.0 all-gather.18
  580.8 8.7 reduce-scatter.19
  599.4 10.5 all-gather.20
  620.4 38.7 reduce-scatter.21
  673.0 31.4 all-reduce.6
  707.1 15.9 reduce-scatter.23
  728.4 40.8 all-gather.22
  771.4 53.7 all-gather.14
  827.9 8.7 reduce-scatter.25
  839.4 9.9 reduce-scatter.15
  875.2 758.6 all-reduce.8
where the time goes:
time: 1680 us; the launch traced here: 1670 us
  waiting for transfers between devices  1160 us (69%)
  blocking collectives  157 us (9%)
  local copies, waits for them, and re-layouts  131 us (8%)
  matrix products  123 us (7%)
  other arithmetic  88.9 us (5%)
    psum x1, waiting for transfers between devices, body(): lax.psum(grad_query.astype(jnp.bfloat16), 'group').astype(jnp.float32)  632 us
    reduce_scatter x3, waiting for transfers between devices, reduce_rows(): lax.psum_scatter(term(jnp.int32(0), lax.axis_size('row') * rows), 'row',...  184 us
    all_gather x3, waiting for transfers between devices, gather_blocks(): return lax.all_gather(values, 'row', axis=0, tiled=True)  104 us
    all_gather x1, waiting for transfers between devices, body(): gathered_pair = lax.all_gather(d_pair, 'row', axis=0, tiled=True)  97.8 us
    reduce_scatter x1, waiting for transfers between devices, body(): lax.psum_scatter(jnp.dot(gathered_two, w_pair, preferred_element_type=jnp...  84.6 us
    psum x1, blocking collectives, body(): lax.psum((query_gain_part, key_gain_part), ('group', 'row', 'col'))  44 us
    psum x1, blocking collectives, body(): lax.psum(grad_head_gate.astype(jnp.bfloat16), 'group').astype(jnp.float32)  37.7 us
    psum x1, blocking collectives, body(): lax.psum((norm_gain_part, ffn_gain_part), ('group', 'col'))  34.1 us
  transfers between devices with their start and end apart: 19, of which 14 were waited for; matrix products, arithmetic and copies ran while one was open for 10% of the time, Pallas kernels for 0%

commit v1 on v0

--- a/solution.py
+++ b/solution.py
@@ -6,6 +6,10 @@
 EPS = 1e-06
 THETA = 1000000.0
 NEGATIVE = -1e30
+
+
+def _refer_modes(local, axis_id):
+    return jax.lax.all_gather(local, axis_id).sum(axis=0)
 
 
 def places(lengths_group, count):
@@ -348,7 +352,7 @@
         lax.psum(grad_query.astype(jnp.bfloat16), "group").astype(jnp.float32),
         lax.psum(grad_key.astype(jnp.bfloat16), "group").astype(jnp.float32),
         lax.psum(grad_value.astype(jnp.bfloat16), "group").astype(jnp.float32),
-        lax.psum(grad_head_gate.astype(jnp.bfloat16), "group").astype(jnp.float32),
+        _refer_modes(grad_head_gate.astype(jnp.bfloat16), "group").astype(jnp.float32),
         lax.psum(grad_out_w.astype(jnp.bfloat16), "group").astype(jnp.float32),
         lax.psum(grad_gate.astype(jnp.bfloat16), "group").astype(jnp.float32),
         lax.psum(grad_up.astype(jnp.bfloat16), "group").astype(jnp.float32),

time: 1680 us -> 1680 us (level)
    psum x1 -> x0, blocking collectives: 37.7 us -> none  [body(): lax.psum(grad_head_gate.astype(jnp.bfloat16), 'group').astype(jnp.float32)]
    all_gather x0 -> x1, blocking collectives: none -> 32.4 us  [_refer_modes(): return jax.lax.all_gather(local, axis_id).sum(axis=0)]
where the time goes in v1:
time: 1680 us; the launch traced here: 1670 us
  waiting for transfers between devices  1160 us (69%)
  blocking collectives  152 us (9%)
  local copies, waits for them, and re-layouts  131 us (8%)
  matrix products  123 us (7%)
  other arithmetic  89 us (5%)
    psum x1, waiting for transfers between devices, body(): lax.psum(grad_query.astype(jnp.bfloat16), 'group').astype(jnp.float32)  638 us
    reduce_scatter x3, waiting for transfers between devices, reduce_rows(): lax.psum_scatter(term(jnp.int32(0), lax.axis_size('row') * rows), 'row',...  184 us
    all_gather x3, waiting for transfers between devices, gather_blocks(): return lax.all_gather(values, 'row', axis=0, tiled=True)  104 us
    all_gather x1, waiting for transfers between devices, body(): gathered_pair = lax.all_gather(d_pair, 'row', axis=0, tiled=True)  97.8 us
    reduce_scatter x1, waiting for transfers between devices, body(): lax.psum_scatter(jnp.dot(gathered_two, w_pair, preferred_element_type=jnp...  84.6 us
    psum x1, blocking collectives, body(): lax.psum((query_gain_part, key_gain_part), ('group', 'row', 'col'))  43.8 us
    psum x1, blocking collectives, body(): lax.psum((norm_gain_part, ffn_gain_part), ('group', 'col'))  34 us
    unnamed x147, local copies, waits for them, and re-layouts  33.7 us
  transfers between devices with their start and end apart: 19, of which 14 were waited for; matrix products, arithmetic and copies ran while one was open for 10% of the time, Pallas kernels for 0%

profile of v1, /device:TPU:0, one launch (start us, length us, event | category | flops | bytes accessed | tf_op | source)
XLA Modules:
  0.0 1673.5 jit_solution(17470660931360968400)
XLA Ops:
  18.3 10.4 all-gather.10.cloned.1.call-done
  34.1 8.5 fusion.52
  52.2 60.9 %reduce-scatter.28.cloned.1.call-done = f32[320,2056]{1,0:T(8,128)} async-done(((f32[640,2056]{1,0:T(8,128)}), f32[320,2056]{1,0:T(8,128)}) %reduce-scatter.28.cloned.1.call-update) | async-done | bytes 2631696 | tf_op jit(solution)/shard_map/reduce_scatter | solution.py:67
  134.4 10.9 all_gather.37
  149.0 10.0 all_gather.38
  185.8 25.1 %all-gather.12.cloned.1.call-done = bf16[640,1024]{1,0:T(8,128)(2,1)} async-done(((bf16[320,1024]{1,0:T(8,128)(2,1)}), bf16[640,1024]{1,0:T(8,128)(2,1)}) %all-gather.12.cloned.1.call-update) | async-done | bytes 1310736 | tf_op jit(solution)/shard_map/all_gather | solution.py:63
  220.8 8.9 reduce-scatter.12.cloned.1.call-done
  245.0 6.4 constant_dynamic-update-slice_fusion
  251.4 15.2 convolution_convert_fusion.1
  266.7 10.7 fusion.84
  277.4 84.6 %reduce-scatter.14.cloned.1.call-done = bf16[320,6144]{1,0:T(8,128)(2,1)} async-done(((bf16[640,6144]{1,0:T(8,128)(2,1)}), bf16[320,6144]{1,0:T(8,128)(2,1)}) %reduce-scatter.14.cloned.1.call-update) | async-done | bytes 3932176 | tf_op jit(solution)/shard_map/reduce_scatter | solution.py:197
  368.3 90.8 %reduce-scatter.18.cloned.1.call-done = f32[320,3072]{1,0:T(8,128)} async-done(((f32[640,3072]{1,0:T(8,128)}), f32[320,3072]{1,0:T(8,128)}) %reduce-scatter.18.cloned.1.call-update) | async-done | bytes 3932176 | tf_op jit(solution)/shard_map/reduce_scatter | solution.py:67
  459.1 6.7 multiply_convert_fusion.1
  468.5 97.8 %all-gather.20.cloned.1.call-done = bf16[640,6144]{1,0:T(8,128)(2,1)} async-done(((bf16[320,6144]{1,0:T(8,128)(2,1)}), bf16[640,6144]{1,0:T(8,128)(2,1)}) %all-gather.20.cloned.1.call-update) | async-done | bytes 7864336 | tf_op jit(solution)/shard_map/all_gather | solution.py:228
  566.3 14.4 convolution_convert_fusion.6
  580.8 8.9 reduce-scatter.20.cloned.1.call-done
  599.3 10.7 all-gather.22.cloned.1.call-done
  626.7 32.6 %reduce-scatter.22.cloned.1.call-done = f32[320,1024]{1,0:T(8,128)} async-done(((f32[640,1024]{1,0:T(8,128)}), f32[320,1024]{1,0:T(8,128)}) %reduce-scatter.22.cloned.1.call-update) | async-done | bytes 1310736 | tf_op jit(solution)/shard_map/reduce_scatter | solution.py:67
  711.1 12.1 reduce-scatter.24.cloned.1.call-done
  728.9 40.4 %all-gather.24.cloned.1.call-done = bf16[640,2056]{1,0:T(8,128)(2,1)} async-done(((bf16[320,2056]{1,0:T(8,128)(2,1)}), bf16[640,2056]{1,0:T(8,128)(2,1)}) %all-gather.24.cloned.1.call-update) | async-done | bytes 2631696 | tf_op jit(solution)/shard_map/all_gather | solution.py:63
  769.3 9.3 gather_fusion.5
  778.6 7.7 convolution_convert_fusion.5
  786.8 38.4 %all-gather.16.cloned.1.call-done = bf16[640,3072]{1,0:T(8,128)(2,1)} async-done(((bf16[320,3072]{1,0:T(8,128)(2,1)}), bf16[640,3072]{1,0:T(8,128)(2,1)}) %all-gather.16.cloned.1.call-update) | async-done | bytes 3932176 | tf_op jit(solution)/shard_map/all_gather | solution.py:63
  825.2 9.3 convolution_convert_fusion.7
  834.5 9.6 convolution_convert_fusion.2
  844.1 14.4 convolution_convert_fusion
  874.8 43.8 %all-reduce.1 = (f32[128]{0:T(128)}, f32[128]{0:T(128)}) all-reduce(f32[128]{0:T(128)S(1)} %bitcast_reduce_fusion, f32[128]{0:T(128)S(1)} %get-tuple-element.197), channel_id=1, replica_groups=mesh['group'=8,'row'=2,'col'=2] {'group','row','col'}, use_global_device_ids=true, to_apply=%region_37.38 | all-reduce | flops 256 | bytes 2048 | tf_op jit(solution)/shard_map/psum | solution.py:344
  918.6 32.4 %all-gather = bf16[8192,8]{0,1:T(8,128)(2,1)S(1)} all-gather(bf16[1024,8]{0,1:T(8,128)(2,1)S(1)} %slice-done.6), channel_id=2, replica_groups=mesh['group'=8,'row'=2,'col'=2] {'group'}, dimensions={0}, use_global_device_ids=true | all-gather | bytes 147456 | tf_op jit(solution)/shard_map/all_gather | solution.py:12
  958.1 34.0 %all-reduce.2 = (f32[1024]{0:T(1024)}, f32[1024]{0:T(1024)}) all-reduce(f32[1024]{0:T(1024)S(1)} %get-tuple-element.199, f32[1024]{0:T(1024)S(1)} %get-tuple-element.195), channel_id=1, replica_groups=mesh['group'=8,'row'=2,'col'=2] {'group','col'}, use_global_device_ids=true, to_apply=%region_30.31 | all-reduce | flops 2048 | bytes 16384 | tf_op jit(solution)/shard_map/psum | solution.py:343
  995.7 638.1 %all-reduce.9.cloned.1.call-done = (bf16[1024,1024]{0,1:T(8,128)(2,1)}, bf16[1024,512]{0,1:T(8,128)(2,1)}, bf16[1024,512]{0,1:T(8,128)(2,1)}, bf16[1024,1024]{1,...) async-done(((bf16[1024,1024]{0,1:T(8,128)(2,1)}, bf16[1024,512]{0,1:T(8,128)(2,1)}, ...) | async-done | bytes 25165840 | tf_op jit(solution)/shard_map/psum | solution.py:352
  1644.6 9.4 convert_element_type.181
  1654.0 6.4 convert_element_type.182
  (314 shorter events, 239.3 us)
Async XLA Ops:
  7.2 209.6 %copy-start = (bf16[1024,1024]{1,0:T(8,128)(2,1)S(1)}, bf16[1024,1024]{1,0:T(8,128)(2,1)}, u32[]{:S(2)}) copy-start(bf16[1024,1024]{1,0:T(8,128)(2,1)} %param.24) | copy-start | bytes 6291460
  7.2 21.5 %all-gather.10.cloned.1.call-start = ((), (), s32[]{:S(2)}) async-start(), calls=%async_computation.9 | async-start | bytes 1966080 | tf_op jit(solution)/shard_map/all_gather | solution.py:59
  17.3 95.9 %reduce-scatter.28.cloned.1.call-start = ((), (), s32[]{:S(2)}) async-start(), calls=%async_computation.25 | async-start | bytes 8355840 | tf_op jit(solution)/shard_map/reduce_scatter | solution.py:67
  42.6 168.3 %all-gather.12.cloned.1.call-start = ((), (), s32[]{:S(2)}) async-start(), calls=%async_computation.10 | async-start | bytes 1966080 | tf_op jit(solution)/shard_map/all_gather | solution.py:63
  128.6 16.6 copy-start.36
  130.6 16.8 %copy-start.58 = (f32[128]{0:T(128)S(1)}, f32[128]{0:T(128)}, u32[]{:S(2)}) copy-start(f32[128]{0:T(128)} %param.23) | copy-start | bytes 1540
  185.7 43.9 %reduce-scatter.12.cloned.1.call-start = ((), (), s32[]{:S(2)}) async-start(), calls=%async_computation.11 | async-start | bytes 1966080 | tf_op jit(solution)/shard_map/reduce_scatter | solution.py:73
  220.7 30.7 %all-gather.14.cloned.1.call-start = ((), (), s32[]{:S(2)}) async-start(), calls=%async_computation.12 | async-start | bytes 1966080 | tf_op jit(solution)/shard_map/all_gather | solution.py:59
  238.2 28.5 %all-gather.18.cloned.1.call-start = ((), (), s32[]{:S(2)}) async-start(), calls=%async_computation.16 | async-start | bytes 1966080 | tf_op jit(solution)/shard_map/all_gather | solution.py:59
  238.8 123.3 %reduce-scatter.14.cloned.1.call-start = ((), (), s32[]{:S(2)}) async-start(), calls=%async_computation.13 | async-start | bytes 11796480 | tf_op jit(solution)/shard_map/reduce_scatter | solution.py:197
  266.6 192.5 %reduce-scatter.18.cloned.1.call-start = ((), (), s32[]{:S(2)}) async-start(), calls=%async_computation.17 | async-start | bytes 11796480 | tf_op jit(solution)/shard_map/reduce_scatter | solution.py:67
  277.4 288.9 %all-gather.20.cloned.1.call-start = ((), (), s32[]{:S(2)}) async-start(), calls=%async_computation.18 | async-start | bytes 11796480 | tf_op jit(solution)/shard_map/all_gather | solution.py:228
  468.0 121.6 %reduce-scatter.20.cloned.1.call-start = ((), (), s32[]{:S(2)}) async-start(), calls=%async_computation.19 | async-start | bytes 1966080 | tf_op jit(solution)/shard_map/reduce_scatter | solution.py:73
  580.7 29.3 %all-gather.22.cloned.1.call-start = ((), (), s32[]{:S(2)}) async-start(), calls=%async_computation.20 | async-start | bytes 1966080 | tf_op jit(solution)/shard_map/all_gather | solution.py:59
  599.2 60.0 %reduce-scatter.22.cloned.1.call-start = ((), (), s32[]{:S(2)}) async-start(), calls=%async_computation.21 | async-start | bytes 3932160 | tf_op jit(solution)/shard_map/reduce_scatter | solution.py:67
  620.3 88.9 %all-reduce.7.cloned.1.call-start = ((), (), s32[]{:S(2)}) async-start(), calls=%async_computation.26 | async-start | bytes 1310720
  672.8 50.3 %reduce-scatter.24.cloned.1.call-start = ((), (), s32[]{:S(2)}) async-start(), calls=%async_computation.22 | async-start | bytes 983040 | tf_op jit(solution)/shard_map/reduce_scatter | solution.py:301
  695.8 73.5 %all-gather.24.cloned.1.call-start = ((), (), s32[]{:S(2)}) async-start(), calls=%async_computation.23 | async-start | bytes 4177920 | tf_op jit(solution)/shard_map/all_gather | solution.py:63
  704.8 18.4 %copy-start.32 = (f32[320,128]{1,0:T(8,128)S(1)}, f32[320,128]{1,0:T(8,128)}, u32[]{:S(2)}) copy-start(f32[320,128]{1,0:T(8,128)} %copy.217) | copy-start | bytes 491524
  728.3 96.9 %all-gather.16.cloned.1.call-start = ((), (), s32[]{:S(2)}) async-start(), calls=%async_computation.14 | async-start | bytes 5898240 | tf_op jit(solution)/shard_map/all_gather | solution.py:63
  728.9 49.8 %copy-start.50 = (bf16[1024,8]{1,0:T(8,128)(2,1)S(1)}, bf16[1024,8]{1,0:T(8,128)(2,1)}, u32[]{:S(2)}) copy-start(bf16[1024,8]{1,0:T(8,128)(2,1)} %copy.209) | copy-start | bytes 49156
  728.9 49.7 %copy-start.62 = (bf16[1024,512]{1,0:T(8,128)(2,1)S(1)}, bf16[1024,512]{1,0:T(8,128)(2,1)}, u32[]{:S(2)}) copy-start(bf16[1024,512]{1,0:T(8,128)(2,1)} %param.20) | copy-start | bytes 3145732
  728.9 222.8 %reduce-scatter.26.cloned.1.call-start = ((), (), s32[]{:S(2)}) async-start(), calls=%async_computation.24 | async-start | bytes 1966080 | tf_op jit(solution)/shard_map/reduce_scatter | solution.py:73
  786.3 205.8 %reduce-scatter.16.cloned.1.call-start = ((), (), s32[]{:S(2)}) async-start(), calls=%async_computation.15 | async-start | bytes 1966080 | tf_op jit(solution)/shard_map/reduce_scatter | solution.py:73
  834.5 799.4 %all-reduce.9.cloned.1.call-start = ((), (), s32[]{:S(2)}) async-start(), calls=%async_computation.27 | async-start | bytes 50331648 | tf_op jit(solution)/shard_map/psum | solution.py:352
  874.7 43.9 %slice-start.6 = ((bf16[1024,2056]{0,1:T(8,128)(2,1)}), bf16[1024,8]{0,1:T(8,128)(2,1)S(1)}, s32[]{:S(2)}) async-start(bf16[1024,2056]{0,1:T(8,128)(2,1)} %copy-done.25), calls=%async_computation.34 | async-start | bytes 32768 | tf_op jit(solution)/shard_map/slice | solution.py:350
  874.7 76.9 %copy-start.52 = (f32[1024]{0:T(1024)S(1)}, f32[1024]{0:T(1024)}, u32[]{:S(2)}) copy-start(f32[1024]{0:T(1024)} %param.17) | copy-start | bytes 12292
  874.7 76.9 %copy-start.54 = (f32[320]{0:T(512)S(1)}, f32[320]{0:T(512)}, u32[]{:S(2)}) copy-start(f32[320]{0:T(512)} %copy-done.53) | copy-start | bytes 3844
  874.7 117.4 %copy-start.18 = (bf16[320,1024]{1,0:T(8,128)(2,1)S(1)}, bf16[320,1024]{1,0:T(8,128)(2,1)}, u32[]{:S(2)}) copy-start(bf16[320,1024]{1,0:T(8,128)(2,1)} %reduce-scatter.20.cloned.1.call-done) | copy-start | bytes 1966084
  874.7 117.4 %copy-start.56 = (f32[320]{0:T(512)S(1)}, f32[320]{0:T(512)}, u32[]{:S(2)}) copy-start(f32[320]{0:T(512)} %copy-done.55) | copy-start | bytes 3844
  874.7 117.4 %copy-start.10 = (bf16[320,1024]{1,0:T(8,128)(2,1)S(1)}, bf16[320,1024]{1,0:T(8,128)(2,1)}, u32[]{:S(2)}) copy-start(bf16[320,1024]{1,0:T(8,128)(2,1)} %reduce-scatter.12.cloned.1.call-done) | copy-start | bytes 1966084
  874.8 117.4 %copy-start.17 = (bf16[320,1024]{1,0:T(8,128)(2,1)S(1)}, bf16[320,1024]{1,0:T(8,128)(2,1)}, u32[]{:S(2)}) copy-start(bf16[320,1024]{1,0:T(8,128)(2,1)} %param.29) | copy-start | bytes 1966084
  (58 other events, 243.5 us)
Sparse Core Ops, SparseCore 0:
  17.4 11.2 all-gather.9
  42.7 70.4 reduce-scatter.27
  185.8 24.9 all-gather.11
  220.9 8.7 reduce-scatter.11
  238.3 10.6 all-gather.13
  250.5 10.5 all-gather.17
  266.7 95.2 reduce-scatter.13
  364.9 94.1 reduce-scatter.17
  468.1 98.0 all-gather.19
  580.8 8.7 reduce-scatter.19
  599.4 10.5 all-gather.21
  620.4 38.7 reduce-scatter.21
  673.0 31.4 all-reduce.6
  707.1 15.9 reduce-scatter.23
  728.4 40.8 all-gather.23
  771.4 53.7 all-gather.15
  827.9 8.7 reduce-scatter.25
  839.4 9.9 reduce-scatter.15
  874.9 758.9 all-reduce.8
